TPU v7x, 32 devices: a whole 2x2x4 slice. The times are simulated.
32 devices in a mesh: dp: 8 (over z, x), seq: 4 (over y, core).
Axes of the slice: x: 2, y: 2, z: 4, core: 2. Of those that a mesh axis runs over, the one named last changes fastest.
Arguments:
- tiles: bfloat16 [8, 1536, 1536], P('dp', 'seq'), may hold values from -24 to 24
- tile_counts: int32 [8, 4], P('dp'), may hold values from 96 to 384, as said below
- norm_gain: float32 [1536], replicated, may hold values from 0.5 to 8
- qkv_weight: bfloat16 [1536, 2304], P('dp'), may hold values from -1 to 1
Outputs:
- context: bfloat16 [8, 1536, 768], P('dp', 'seq')
Inputs may be any that keep to these rules, and one draw needn't show every extreme that they name: `tile_counts`: every slide has one block with exactly 384 tissue tiles.
All inputs are finite; a program needn't handle non-finite values.
Results may differ from a plain program's by a relative error of at most 0.017.
The roundings to bfloat16 on the way count: a program that leaves them out, or rounds other values in their place, can miss the bound.
Values may be sent and summed in bfloat16 or wider, within the bound.
No kernel may reach another device: no remote copies, remote signals or barrier semaphores. Data moves between devices by JAX's collectives and lax.ppermute only.
A program may use at most 64 MiB of HBM per device.

v0:
```python
import jax
import jax.numpy as jnp
from jax import lax
from jax.sharding import PartitionSpec as P

HEADS = 6
MID_RATE = 4
NEG = -1e30
EPS = 1e-05


def from_partner(value, axis, bit):
    mask = 2**bit
    pairs = [(source, source ^ mask) for source in range(lax.axis_size(axis))]
    return lax.ppermute(value, axis, pairs)


def layer_norm(rows_in, gain):
    floats = rows_in.astype(jnp.float32)
    center = floats - jnp.mean(floats, axis=-1, keepdims=True)
    spread_sq = jnp.mean(center * center, axis=-1, keepdims=True)
    return (center * lax.rsqrt(spread_sq + EPS) * gain).astype(jnp.bfloat16)


def sample_rows(array, stride):
    shaped = array.reshape((array.shape[0] // stride, stride) + array.shape[1:])
    return jnp.stack([shaped[:, head_idx % stride, head_idx] for head_idx in range(array.shape[1])])


def attend(queries, keys, values_in, key_live, scale):
    scores = (
        jnp.einsum("hsqd,hskd->hsqk", queries, keys, preferred_element_type=jnp.float32) * scale
    )
    scores = jnp.where(key_live[:, :, None, :], scores, NEG)
    top = jnp.max(scores, axis=-1)
    expo = jnp.exp(scores - top[..., None])
    denom = jnp.sum(expo, axis=-1)
    weights = (expo / denom[..., None]).astype(jnp.bfloat16)
    result = jnp.einsum("hsqk,hskd->hsqd", weights, values_in, preferred_element_type=jnp.float32)
    return (result, top + jnp.log(denom))


def spread(result, log_total, stride):
    heads_n = result.shape[0]
    count_n = result.shape[1]
    onehot = (
        jnp.arange(stride, dtype=jnp.int32)[None, :]
        == (jnp.arange(heads_n, dtype=jnp.int32) % stride)[:, None]
    )
    full_ctx = (result[:, :, None, :] * onehot[:, None, :, None].astype(result.dtype)).reshape(
        heads_n, count_n * stride, result.shape[2]
    )
    chosen = jnp.broadcast_to(onehot[:, None, :], (heads_n, count_n, stride)).reshape(
        heads_n, count_n * stride
    )
    full_lt = jnp.where(chosen, jnp.repeat(log_total, stride, axis=1), NEG)
    return (full_ctx, full_lt)


def combine(contexts, totals):
    stacked_lt = jnp.stack(totals)
    top = jnp.max(stacked_lt, axis=0)
    wts = jnp.exp(stacked_lt - top)
    stacked_ctx = jnp.stack(contexts)
    return jnp.sum(wts[..., None] * stacked_ctx, axis=0) / jnp.sum(wts, axis=0)[..., None]


def key_alive(owners, within, counts, stride, heads_n):
    seq_n = counts.shape[0]
    owner_count = jnp.sum(
        jnp.where(
            owners[:, None] == jnp.arange(seq_n, dtype=jnp.int32)[None, :], counts[None, :], 0
        ),
        axis=1,
    )
    offsets = jnp.arange(heads_n, dtype=jnp.int32) % stride
    slots = offsets[:, None] + stride * within[None, :]
    return slots < owner_count[None, :]


def sampled_attention(queries, gathered, alive, stride, scale):
    heads_n = queries.shape[0]
    per_dev = queries.shape[1]
    result, log_total = attend(
        queries[:, None], gathered[0][:, None], gathered[1][:, None], alive[:, None], scale
    )
    return spread(
        result.reshape(heads_n, per_dev, result.shape[3]),
        log_total.reshape(heads_n, per_dev),
        stride,
    )


def local(tiles, tile_counts, norm_gain, qkv_weight):
    rows_in = tiles[0]
    counts = tile_counts[0]
    tok_dev = rows_in.shape[0]
    seq_n = lax.axis_size("seq")
    my_index = lax.axis_index("seq")
    dev_ids = jnp.arange(seq_n, dtype=jnp.int32)
    my_count = jnp.sum(jnp.where(dev_ids == my_index, counts, 0))
    is_live = jnp.arange(tok_dev, dtype=jnp.int32) < my_count
    normed = layer_norm(rows_in, norm_gain)
    width3 = qkv_weight.shape[1]
    width = width3 // 3
    heads_n = HEADS
    head_dim = width // heads_n
    scale = head_dim ** (-0.5)
    qkv = jnp.dot(
        normed,
        lax.all_gather(qkv_weight, "dp", axis=0, tiled=True),
        preferred_element_type=jnp.float32,
    ).astype(jnp.bfloat16)
    queries = qkv[:, :width].reshape(tok_dev, heads_n, head_dim)
    keys = qkv[:, width : 2 * width].reshape(tok_dev, heads_n, head_dim)
    values_in = qkv[:, 2 * width :].reshape(tok_dev, heads_n, head_dim)
    local_live = jnp.broadcast_to(is_live[None, None, :], (heads_n, 1, tok_dev))
    local_ctx, local_lt = attend(
        queries.transpose(1, 0, 2)[:, None],
        keys.transpose(1, 0, 2)[:, None],
        values_in.transpose(1, 0, 2)[:, None],
        local_live,
        scale,
    )
    local_ctx = local_ctx.reshape(heads_n, tok_dev, head_dim)
    local_lt = local_lt.reshape(heads_n, tok_dev)
    mid_stride = MID_RATE
    mid_rows = tok_dev // mid_stride
    q_mid = sample_rows(queries, mid_stride)
    kv_mid = jnp.stack([sample_rows(keys, mid_stride), sample_rows(values_in, mid_stride)])
    bit_count = MID_RATE.bit_length() - 1
    bit_order = list(range(bit_count))
    mid_keys = kv_mid
    source_ids = jnp.reshape(my_index, (1,))
    for bit_pos in bit_order:
        partner_keys = from_partner(mid_keys, "seq", bit_pos)
        mid_keys = jnp.concatenate([mid_keys, partner_keys], axis=2)
        source_ids = jnp.concatenate([source_ids, source_ids ^ 1 << bit_pos])
    mid_owners = jnp.repeat(source_ids, mid_rows, total_repeat_length=mid_stride * mid_rows)
    mid_within = jnp.tile(jnp.arange(mid_rows, dtype=jnp.int32), mid_stride)
    mid_alive = key_alive(mid_owners, mid_within, counts, mid_stride, heads_n)
    mid_ctx, mid_lt = sampled_attention(q_mid, mid_keys, mid_alive, mid_stride, scale)
    wide_rows = tok_dev // seq_n
    q_wide = sample_rows(queries, seq_n)
    kv_wide = jnp.stack([sample_rows(keys, seq_n), sample_rows(values_in, seq_n)])
    wide_keys = lax.all_gather(kv_wide, "seq", axis=2, tiled=True)
    wide_owners = jnp.arange(seq_n * wide_rows, dtype=jnp.int32) // wide_rows
    wide_within = jnp.arange(seq_n * wide_rows, dtype=jnp.int32) % wide_rows
    wide_alive = key_alive(wide_owners, wide_within, counts, seq_n, heads_n)
    wide_ctx, wide_lt = sampled_attention(q_wide, wide_keys, wide_alive, seq_n, scale)
    mixed = combine([local_ctx, mid_ctx, wide_ctx], [local_lt, mid_lt, wide_lt])
    mixed = jnp.where(is_live[None, :, None], mixed, 0.0)
    return mixed.transpose(1, 0, 2).reshape(tok_dev, width).astype(jnp.bfloat16)[None]


def solution(mesh):
    return jax.shard_map(
        local,
        mesh=mesh,
        in_specs=(P("dp", "seq", None), P("dp", None), P(), P("dp", None)),
        out_specs=P("dp", "seq", None),
        check_vma=False,
    )
```

profile of v0, /device:TPU:0, one launch (start us, length us, event | category | flops | bytes accessed | tf_op | source)
XLA Modules:
  0.0 174.4 jit_solution(12791462369132801549)
XLA Ops:
  6.5 0.7 all-gather.3.cloned.1.call-update
  7.4 0.6 iota_compare_fusion.2
  8.3 1.4 fusion.37
  9.7 1.2 iota_compare_fusion.3
  10.9 0.7 fusion.47
  11.6 2.1 %add_select_fusion = (s32[384]{0:T(512)S(1)}, s32[384]{0:T(512)S(1)}) fusion(pred[384]{0:T(512)(128)(4,1)} %constant.173, pred[384]{0:T(512)(128)(4,1)} %constant.174, pred[384]{0:T(512)(128)(4,1)} %constant.175, s32[]{:T(128)} %axis_index.12, s32[]{:T(128)} %bitcast.10, s32[]{:T(128)} %bitcast.9, s32[]{:T(128)} %bitcast.8), kind=kLoop, calls=%fused_computation.103 | loop fusion | flops 4224 | bytes 4240 | tf_op jit(solution)/shard_map/jit(floor_divide)/jit(_where)/select_n | solution.py:147
  13.6 0.7 select_reduce_fusion.1
  14.6 0.5 fusion.6
  15.1 0.7 add_compare_fusion.1
  15.8 104.8 %all-gather.3.cloned.1.call-done = bf16[1536,2304]{1,0:T(8,128)(2,1)} async-done(((bf16[192,2304]{1,0:T(8,128)(2,1)}), bf16[1536,2304]{1,0:T(8,128)(2,1)}) %all-gather.3.cloned.1.call-update) | async-done | bytes 7077904 | tf_op jit(solution)/shard_map/all_gather | solution.py:111
  120.6 6.1 %convolution_convert_fusion = bf16[384,2304]{1,0:T(8,128)(2,1)S(1)} fusion(bf16[1536,2304]{1,0:T(8,128)(2,1)} %all-gather.3.cloned.1.call-done, bf16[1,384,1536]{2,1,0:T(8,128)(2,1)S(1)} %copy-done, f32[1536]{0:T(1024)S(1)} %copy-done.8, f32[384]{0:T(512)S(1)} %add_rsqrt_fusion, f32[384]{0:T(512)S(1)} %broadcast_multiply_fusion.2), kind=kOutput, calls=%fused_computation | convolution fusion | flops 2721742848 | bytes 10036224 | tf_op jit(solution)/shard_map/dot_general | solution.py:109
  126.8 0.7 reshape_reshape.14
  127.7 0.7 reshape_reshape.13
  128.9 0.7 pad_maximum_fusion.2
  129.9 0.7 reshape_reshape.12
  131.2 0.9 fusion.44
  132.8 1.1 copy.103
  134.0 0.7 fusion.1
  134.7 0.8 fusion.2
  135.5 1.0 pad_maximum_fusion.1
  136.5 1.6 collective-permute-start.1
  138.2 1.3 fusion.10
  139.5 17.2 %collective-permute-done.1 = bf16[2,6,192,128]{3,2,1,0:T(8,128)(2,1)S(1)} collective-permute-done((bf16[2,6,192,128]{3,2,1,0:T(8,128)(2,1)S(1)}, bf16[2,6,192,128]{3,2,1,0:T(8,128)(2,1)S(1)}, u32[]{:S(2)}, u32[]{:S(2)}) %collective-permute-start.1) | collective-permute-done | bytes 589856 | tf_op jit(solution)/shard_map/ppermute | solution.py:15
  156.7 1.0 pad_maximum_fusion
  157.8 0.5 fusion.48
  158.6 0.5 fusion.22
  159.2 1.5 fusion.49
  162.2 1.4 fusion.21
  164.0 0.4 broadcast_multiply_fusion.1
  164.5 1.2 fusion
  165.7 0.4 fusion.15
  166.5 1.1 copy.106
  (74 shorter events, 5.6 us)
Async XLA Ops:
  6.5 7.9 %copy-start = (bf16[1,384,1536]{2,1,0:T(8,128)(2,1)S(1)}, bf16[1,384,1536]{2,1,0:T(8,128)(2,1)}, u32[]{:S(2)}) copy-start(bf16[1,384,1536]{2,1,0:T(8,128)(2,1)} %param.6) | copy-start | bytes 3538948
  6.5 114.0 %copy-start.8 = (f32[1536]{0:T(1024)S(1)}, f32[1536]{0:T(1024)}, u32[]{:S(2)}) copy-start(f32[1536]{0:T(1024)} %param.8) | copy-start | bytes 18436
  6.5 114.0 %all-gather.3.cloned.1.call-start = ((), (), s32[]{:S(2)}) async-start(), calls=%async_computation | async-start | bytes 7962624 | tf_op jit(solution)/shard_map/all_gather | solution.py:111
  7.3 152.0 %all-gather.5.cloned.1.call-start = ((), (), s32[]{:S(2)}) async-start(), calls=%async_computation.1 | async-start | bytes 1474560 | tf_op jit(solution)/shard_map/all_gather | solution.py:146
  129.6 5.9 %collective-permute-start = (bf16[2,6,96,128]{3,2,1,0:T(8,128)(2,1)}, bf16[2,6,96,128]{3,2,1,0:T(8,128)(2,1)}, u32[]{:S(2)}, u32[]{:S(2)}) collective-permute-start(bf16[2,6,96,128]{3,2,1,0:T(8,128)(2,1)} %pad_maximum_fusion.2), channel_id=1, source_target_pairs={{0,1},{1,0},{2,3},{3,2},{4,5},{5,4},{6,7},{7,6},{8,9},{9,8},{10,11... | collective-permute-start | bytes 884744 | tf_op jit(solution)/shard_map/ppermute | solution.py:15
  132.1 1.7 copy-start.4
  132.1 1.7 copy-start.3
  132.1 1.8 %copy-start.2 = (bf16[96,1,1,128]{3,2,1,0:T(2,128)(2,1)S(1)}, bf16[96,1,1,128]{3,2,1,0:T(2,128)(2,1)}, u32[]{:S(2)}) copy-start(bf16[96,1,1,128]{3,2,1,0:T(2,128)(2,1)} %get-tuple-element.26) | copy-start | bytes 73732
  132.2 1.8 %copy-start.6 = (pred[384]{0:T(512)(128)(4,1)S(1)}, pred[384]{0:T(512)(128)(4,1)}, u32[]{:S(2)}) copy-start(pred[384]{0:T(512)(128)(4,1)} %iota_compare_fusion.3) | copy-start | bytes 1156
  134.7 3.5 %copy-start.1 = (bf16[384,6,128]{2,0,1:T(8,128)(2,1)S(1)}, bf16[384,6,128]{2,0,1:T(8,128)(2,1)}, u32[]{:S(2)}) copy-start(bf16[384,6,128]{2,0,1:T(8,128)(2,1)} %copy.103) | copy-start | bytes 1769476
  136.5 20.2 %collective-permute-start.1 = (bf16[2,6,192,128]{3,2,1,0:T(8,128)(2,1)S(1)}, bf16[2,6,192,128]{3,2,1,0:T(8,128)(2,1)S(1)}, u32[]{:S(2)}, u32[]{:S(2)}) collective-permute-start(bf16[2,6,192,128]{3,2,1,0:T(8,128)(2,1)S(1)} %pad_maximum_fusion.1), channel_id=1, source_target_pairs={{0,2},{1,3},{2,0},{3,1},{4,6},{5,7},{6,4},{7,5},{8,10},{9,11},{10,... | collective-permute-start | bytes 1769480 | tf_op jit(solution)/shard_map/ppermute | solution.py:15
  139.5 18.3 %copy-start.5 = (pred[6,384]{1,0:T(8,128)(4,1)S(1)}, pred[6,384]{1,0:T(8,128)(4,1)}, u32[]{:S(2)}) copy-start(pred[6,384]{1,0:T(8,128)(4,1)} %get-tuple-element.50) | copy-start | bytes 6916
  159.2 2.0 %copy-start.7 = (pred[6,4]{1,0:T(8,128)(4,1)S(1)}, pred[6,4]{1,0:T(8,128)(4,1)}, u32[]{:S(2)}) copy-start(pred[6,4]{1,0:T(8,128)(4,1)} %get-tuple-element.48) | copy-start | bytes 76
Sparse Core Ops, SparseCore 0:
  9.5 110.9 all-gather.2
  129.8 20.2 all-gather.4
where the time goes:
time: 175 us; the launch traced here: 174 us
  waiting for transfers between devices  123 us (70%)
  other arithmetic  14.2 us (8%)
  between operations  13.8 us (8%)
  matrix products  12 us (7%)
  local copies, waits for them, and re-layouts  9.92 us (6%)
    all_gather x1, waiting for transfers between devices, local(): lax.all_gather(qkv_weight, 'dp', axis=0, tiled=True)  105 us
    ppermute x2, waiting for transfers between devices, from_partner(): return lax.ppermute(value, axis, pairs)  17.2 us
    dot_general x1, matrix products, local(): jnp.dot(normed, lax.all_gather(qkv_weight, 'dp', axis=0, tiled=True), pre...  6.07 us
  transfers between devices with their start and end apart: 4, of which 2 were waited for; matrix products, arithmetic and copies ran while one was open for 11% of the time, Pallas kernels for 0%

commit v1 on v0

--- a/solution.py
+++ b/solution.py
@@ -108,7 +108,9 @@
     scale = head_dim ** (-0.5)
     qkv = jnp.dot(
         normed,
-        lax.all_gather(qkv_weight, "dp", axis=0, tiled=True),
+        jnp.concatenate(
+            lax.all_to_all(jnp.stack([qkv_weight] * lax.axis_size("dp")), "dp", 0, 0), axis=0
+        ),
         preferred_element_type=jnp.float32,
     ).astype(jnp.bfloat16)
     queries = qkv[:, :width].reshape(tok_dev, heads_n, head_dim)

time: 175 us -> 229 us (1.31)
  waiting for transfers between devices: 123 us -> 167 us
  starting transfers between devices: 1.66 us -> 9.06 us
  local copies, waits for them, and re-layouts: 9.92 us -> 14.4 us
  other arithmetic: 14.2 us -> 11.9 us
    all_to_all x0 -> x1, waiting for transfers between devices: none -> 149 us  [local(): lax.all_to_all(jnp.stack([qkv_weight] * lax.axis_size('dp')), 'dp', 0, 0)]
    all_gather x1 -> x0, waiting for transfers between devices: 105 us -> none  [local(): lax.all_gather(qkv_weight, 'dp', axis=0, tiled=True)]
    all_to_all x0 -> x1, starting transfers between devices: none -> 7.42 us  [local(): lax.all_to_all(jnp.stack([qkv_weight] * lax.axis_size('dp')), 'dp', 0, 0)]
    another operation x0 -> x1, local copies, waits for them, and re-layouts: none -> 4.56 us  [local(): jnp.stack([qkv_weight] * lax.axis_size('dp'))]
  transfers between devices with their start and end apart: 4 -> 4, of which waited for: 2 -> 2; matrix products, arithmetic and copies ran while one was open for 11% -> 7% of each run, Pallas kernels for 0% -> 0%
where the time goes in v1:
time: 229 us; the launch traced here: 228 us
  waiting for transfers between devices  167 us (73%)
  local copies, waits for them, and re-layouts  14.4 us (6%)
  between operations  13.9 us (6%)
  matrix products  12 us (5%)
  other arithmetic  11.9 us (5%)
  starting transfers between devices  9.06 us (4%)
    all_to_all x1, waiting for transfers between devices, local(): lax.all_to_all(jnp.stack([qkv_weight] * lax.axis_size('dp')), 'dp', 0, 0)  149 us
    ppermute x2, waiting for transfers between devices, from_partner(): return lax.ppermute(value, axis, pairs)  18.2 us
    all_to_all x1, starting transfers between devices, local(): lax.all_to_all(jnp.stack([qkv_weight] * lax.axis_size('dp')), 'dp', 0, 0)  7.42 us
    dot_general x1, matrix products, local(): jnp.dot(normed, jnp.concatenate(lax.all_to_all(jnp.stack([qkv_weight] * l...  6.07 us
  transfers between devices with their start and end apart: 4, of which 2 were waited for; matrix products, arithmetic and copies ran while one was open for 7% of the time, Pallas kernels for 0%

profile of v1, /device:TPU:0, one launch (start us, length us, event | category | flops | bytes accessed | tf_op | source)
XLA Modules:
  0.0 228.3 jit_solution(5045058478346879001)
XLA Ops:
  6.5 4.6 %stack.18 = bf16[8,192,2304]{2,1,0:T(8,128)(2,1)} broadcast(bf16[192,2304]{1,0:T(8,128)(2,1)} %param.9), dimensions={1,2} | broadcast | bytes 7962624 | tf_op jit(solution)/shard_map/stack | solution.py:112
  11.1 7.4 %all-to-all-start = ((bf16[8,192,2304]{2,1,0:T(8,128)(2,1)}), bf16[8,192,2304]{2,1,0:T(8,128)(2,1)}, u32[]{:S(2)}, u32[]{:S(2)}) async-start(bf16[8,192,2304]{2,1,0:T(8,128)(2,1)} %stack.18), calls=%async_computation | async-start | bytes 14155776 | tf_op jit(solution)/shard_map/all_to_all | solution.py:112
  18.7 0.6 iota_compare_fusion.2
  19.6 0.7 fusion.38
  20.3 1.1 iota_compare_fusion.3
  21.5 0.6 fusion.48
  22.1 1.3 add_select_fusion
  23.7 0.5 fusion.8
  24.2 0.7 add_compare_fusion.1
  24.8 148.8 %all-to-all-done = bf16[8,192,2304]{2,1,0:T(8,128)(2,1)} async-done(((bf16[8,192,2304]{2,1,0:T(8,128)(2,1)}), bf16[8,192,2304]{2,1,0:T(8,128)(2,1)}, u32[]{:S(2)}, u32[]{:S(2)}) %all-to-all-start) | async-done | bytes 7077920 | tf_op jit(solution)/shard_map/all_to_all | solution.py:112
  173.6 6.1 %convolution_convert_fusion = bf16[384,2304]{1,0:T(8,128)(2,1)S(1)} fusion(bf16[1536,2304]{1,0:T(8,128)(2,1)} %bitcast.3, bf16[1,384,1536]{2,1,0:T(8,128)(2,1)S(1)} %copy-done, f32[1536]{0:T(1024)S(1)} %copy-done.12, f32[384]{0:T(512)S(1)} %add_rsqrt_fusion, f32[384]{0:T(512)S(1)} %broadcast_multiply_fusion.2), kind=kOutput, calls=%fused_computation | convolution fusion | flops 2721742848 | bytes 10036224 | tf_op jit(solution)/shard_map/dot_general | solution.py:109
  179.8 0.7 reshape_reshape.14
  180.8 0.7 reshape_reshape.13
  181.9 0.7 pad_maximum_fusion.2
  183.0 0.7 reshape_reshape.12
  184.3 0.9 fusion.45
  185.9 1.1 copy.103
  187.0 0.7 fusion.1
  187.7 0.8 fusion.2
  188.6 1.0 pad_maximum_fusion.1
  189.6 1.6 collective-permute-start.1
  191.2 1.3 fusion.10
  192.5 18.2 %collective-permute-done.1 = bf16[2,6,192,128]{3,2,1,0:T(8,128)(2,1)S(1)} collective-permute-done((bf16[2,6,192,128]{3,2,1,0:T(8,128)(2,1)S(1)}, bf16[2,6,192,128]{3,2,1,0:T(8,128)(2,1)S(1)}, u32[]{:S(2)}, u32[]{:S(2)}) %collective-permute-start.1) | collective-permute-done | bytes 589856 | tf_op jit(solution)/shard_map/ppermute | solution.py:15
  210.7 1.0 pad_maximum_fusion
  211.7 0.5 fusion.49
  212.6 0.6 fusion.23
  213.2 1.5 fusion.50
  216.1 1.4 fusion.22
  218.0 0.4 broadcast_multiply_fusion.1
  218.4 1.2 fusion
  219.7 0.4 fusion.16
  220.4 1.1 copy.106
  (82 shorter events, 5.7 us)
Async XLA Ops:
  11.1 8.5 %copy-start.8 = (s32[1,4]{1,0:T(1,128)S(1)}, s32[1,4]{1,0:T(1,128)}, u32[]{:S(2)}) copy-start(s32[1,4]{1,0:T(1,128)} %param.7) | copy-start | bytes 52
  11.1 11.0 %copy-start.9 = (pred[384]{0:T(512)(128)(4,1)S(1)}, pred[384]{0:T(512)(128)(4,1)}, u32[]{:S(2)}) copy-start(pred[384]{0:T(512)(128)(4,1)} %constant.173) | copy-start | bytes 1156
  11.1 11.0 %copy-start.10 = (pred[384]{0:T(512)(128)(4,1)S(1)}, pred[384]{0:T(512)(128)(4,1)}, u32[]{:S(2)}) copy-start(pred[384]{0:T(512)(128)(4,1)} %constant.174) | copy-start | bytes 1156
  11.1 11.0 %copy-start.11 = (pred[384]{0:T(512)(128)(4,1)S(1)}, pred[384]{0:T(512)(128)(4,1)}, u32[]{:S(2)}) copy-start(pred[384]{0:T(512)(128)(4,1)} %constant.175) | copy-start | bytes 1156
  11.1 12.3 %copy-start = (bf16[1,384,1536]{2,1,0:T(8,128)(2,1)S(1)}, bf16[1,384,1536]{2,1,0:T(8,128)(2,1)}, u32[]{:S(2)}) copy-start(bf16[1,384,1536]{2,1,0:T(8,128)(2,1)} %param.6) | copy-start | bytes 3538948
  11.1 162.5 %all-to-all-start = ((bf16[8,192,2304]{2,1,0:T(8,128)(2,1)}), bf16[8,192,2304]{2,1,0:T(8,128)(2,1)}, u32[]{:S(2)}, u32[]{:S(2)}) async-start(bf16[8,192,2304]{2,1,0:T(8,128)(2,1)} %stack.18), calls=%async_computation | async-start | bytes 14155776 | tf_op jit(solution)/shard_map/all_to_all | solution.py:112
  18.5 155.1 %copy-start.12 = (f32[1536]{0:T(1024)S(1)}, f32[1536]{0:T(1024)}, u32[]{:S(2)}) copy-start(f32[1536]{0:T(1024)} %param.8) | copy-start | bytes 18436
  18.5 194.6 %all-gather.2.cloned.1.call-start = ((), (), s32[]{:S(2)}) async-start(), calls=%async_computation.1 | async-start | bytes 1474560 | tf_op jit(solution)/shard_map/all_gather | solution.py:148
  182.7 5.9 %collective-permute-start = (bf16[2,6,96,128]{3,2,1,0:T(8,128)(2,1)}, bf16[2,6,96,128]{3,2,1,0:T(8,128)(2,1)}, u32[]{:S(2)}, u32[]{:S(2)}) collective-permute-start(bf16[2,6,96,128]{3,2,1,0:T(8,128)(2,1)} %pad_maximum_fusion.2), channel_id=1, source_target_pairs={{0,1},{1,0},{2,3},{3,2},{4,5},{5,4},{6,7},{7,6},{8,9},{9,8},{10,11... | collective-permute-start | bytes 884744 | tf_op jit(solution)/shard_map/ppermute | solution.py:15
  185.2 1.7 copy-start.4
  185.2 1.7 copy-start.3
  185.2 1.8 copy-start.2
  185.2 1.8 copy-start.6
  187.7 3.5 %copy-start.1 = (bf16[384,6,128]{2,0,1:T(8,128)(2,1)S(1)}, bf16[384,6,128]{2,0,1:T(8,128)(2,1)}, u32[]{:S(2)}) copy-start(bf16[384,6,128]{2,0,1:T(8,128)(2,1)} %copy.103) | copy-start | bytes 1769476
  189.6 21.1 %collective-permute-start.1 = (bf16[2,6,192,128]{3,2,1,0:T(8,128)(2,1)S(1)}, bf16[2,6,192,128]{3,2,1,0:T(8,128)(2,1)S(1)}, u32[]{:S(2)}, u32[]{:S(2)}) collective-permute-start(bf16[2,6,192,128]{3,2,1,0:T(8,128)(2,1)S(1)} %pad_maximum_fusion.1), channel_id=1, source_target_pairs={{0,2},{1,3},{2,0},{3,1},{4,6},{5,7},{6,4},{7,5},{8,10},{9,11},{10,... | collective-permute-start | bytes 1769480 | tf_op jit(solution)/shard_map/ppermute | solution.py:15
  192.5 19.2 %copy-start.5 = (pred[6,384]{1,0:T(8,128)(4,1)S(1)}, pred[6,384]{1,0:T(8,128)(4,1)}, u32[]{:S(2)}) copy-start(pred[6,384]{1,0:T(8,128)(4,1)} %get-tuple-element.50) | copy-start | bytes 6916
  213.1 2.0 copy-start.7
Sparse Core Ops, SparseCore 0:
  182.8 22.1 all-gather.1
